TPU v7x, 256 devices: a whole 4x4x8 slice. The times are simulated.
256 devices in a mesh: blk: 16 (over x, y_lo, core), lane: 16 (over y_hi, z).
Axes of the slice: x: 4, y: 4 (y_hi: 2, y_lo: 2; y = y_hi * 2 + y_lo), z: 8, core: 2. Of those that a mesh axis runs over, the one named last changes fastest.
Arguments:
- recv_pos: float32 [3, 32768], P(None, ('blk', 'lane')), may hold values from 0 to 6
- recv_angles: float32 [2, 32768], P(None, ('blk', 'lane')), may hold values from -3.140625 to 3.140625
- src_pos: float32 [3, 262144], P(None, ('blk', 'lane')), may hold values from 0 to 6
- src_angles: float32 [2, 262144], P(None, ('blk', 'lane')), may hold values from -3.140625 to 3.140625
- src_area: float32 [262144], P(('blk', 'lane')), may hold values from 0.02 to 0.08
- reemission: float32 [262144], P(('blk', 'lane')), may hold values from 0.1 to 0.9
- incident: bfloat16 [262144, 128], P(('blk', 'lane')), may hold values from 0 to 2
- direct: float32 [32768, 128], P(('blk', 'lane')), may hold values from 0.5 to 1.5
- visible_lists: int32 [16, 16, 16, 16, 4], P('blk', 'lane'), may hold values from 0 to 7, as said below
- visible_counts: int32 [16, 16, 16, 16], P('blk', 'lane'), may hold values from 0 to 4, as said below
Outputs:
- incoming: float32 [32768, 128], P(('blk', 'lane'))
Inputs may be any that keep to these rules, and one draw needn't show every extreme that they name: `visible_lists`: each list names 4 different local source blocks of its device; entries at slots at or past the count are valid but unused. `visible_counts`: some list holds exactly 4 used entries in every draw; the loads differ from device to device.
All inputs are finite; a program needn't handle non-finite values.
Results may differ from a plain program's by a relative error of at most 0.0003.
Values sent between devices are 32-bit elements; how exact they have to be, the bound alone decides.
No kernel may reach another device: no remote copies, remote signals or barrier semaphores. Data moves between devices by JAX's collectives and lax.ppermute only.
A program may use at most 64 MiB of HBM per device.

v0:
```python
import jax
import jax.numpy as jnp
from jax import lax
from jax.sharding import PartitionSpec as P


def shifted(block, axis, distance):
    devices = range(lax.axis_size(axis))
    route = [((i - distance) % len(devices), i) for i in devices]
    return lax.ppermute(block, axis, route)


def normals(angle_rows):
    polar = angle_rows[0]
    azimuth = angle_rows[1]
    return jnp.stack(
        [jnp.sin(polar) * jnp.cos(azimuth), jnp.sin(polar) * jnp.sin(azimuth), jnp.cos(polar)]
    )


def factors(receiver_pos, receiver_dir, source_pos, source_dir, source_area, source_keep):
    offsets = [source_pos[component] - receiver_pos[component] for component in range(3)]
    distance = offsets[0] * offsets[0] + offsets[1] * offsets[1] + offsets[2] * offsets[2]
    facing = jnp.maximum(
        receiver_dir[0] * offsets[0] + receiver_dir[1] * offsets[1] + receiver_dir[2] * offsets[2],
        0.0,
    )
    seen = jnp.maximum(
        -(source_dir[0] * offsets[0] + source_dir[1] * offsets[1] + source_dir[2] * offsets[2]), 0.0
    )
    spread = distance + source_area
    value = source_keep * source_area * facing * seen / (jnp.pi * spread * spread)
    return value.astype(jnp.bfloat16)


def shards(
    recv_pos,
    recv_angles,
    src_pos,
    src_angles,
    src_area,
    reemission,
    incident,
    direct,
    visible_lists,
    visible_counts,
):
    group_count = lax.axis_size("blk")
    lane_count = lax.axis_size("lane")
    block_rows = recv_pos.shape[1]
    bin_count = incident.shape[1]
    source_blocks = src_area.shape[0] // block_rows
    slot_count = visible_lists.shape[-1]
    every_pos, every_angles = (
        lax.all_gather(recv_pos, ("blk", "lane"), axis=1, tiled=True),
        lax.all_gather(recv_angles, ("blk", "lane"), axis=1, tiled=True),
    )
    receiver_pos = every_pos.reshape(3, group_count * lane_count, block_rows)
    receiver_dir = normals(every_angles).reshape(3, group_count * lane_count, block_rows)
    source_pos = src_pos.reshape(3, source_blocks, block_rows)
    source_dir = normals(src_angles).reshape(3, source_blocks, block_rows)
    source_area = src_area.reshape(source_blocks, block_rows)
    source_keep = reemission.reshape(source_blocks, block_rows)
    emission = incident.reshape(source_blocks, block_rows, bin_count)
    my_lists = visible_lists[0, 0]
    my_counts = visible_counts[0, 0]
    group_index = lax.axis_index("blk")
    lane_range = jnp.arange(lane_count, dtype=jnp.int32)
    slot_range = jnp.arange(slot_count, dtype=jnp.int32)

    def slab_of(cycle_step):
        ahead = (group_index - cycle_step - 1) % group_count
        return ahead + 0 * lane_range

    def contribution(cycle_step):
        slabs = slab_of(cycle_step)
        targets = slabs * lane_count + lane_range
        near_pos = jnp.take(receiver_pos, targets, axis=1)
        near_dir = jnp.take(receiver_dir, targets, axis=1)
        chosen = my_lists[slabs, lane_range]
        counts_here = my_counts[slabs, lane_range]
        picked_pos = source_pos[:, chosen]
        picked_dir = source_dir[:, chosen]
        picked_area = source_area[chosen]
        picked_keep = source_keep[chosen]
        picked_flux = emission[chosen]
        values = factors(
            near_pos[:, :, :, None, None],
            near_dir[:, :, :, None, None],
            picked_pos[:, :, None, :, :],
            picked_dir[:, :, None, :, :],
            picked_area[:, None, :, :],
            picked_keep[:, None, :, :],
        )
        live_mask = (slot_range[None, :] < counts_here[:, None])[:, None, :, None]
        values = jnp.where(live_mask, values, jnp.zeros((), jnp.bfloat16))
        return jnp.einsum("jrcs,jcsb->jrb", values, picked_flux, preferred_element_type=jnp.float32)

    def pass_on(running):
        return shifted(running, "blk", 1)

    def cycle_turn(cycle_step, running):
        return pass_on(running + contribution(cycle_step))

    start = jnp.zeros((lane_count, block_rows, bin_count), jnp.float32)
    running = lax.fori_loop(0, group_count - 1, cycle_turn, start)
    running = running + contribution(group_count - 1)
    owned = lax.psum_scatter(
        running.reshape(lane_count * block_rows, bin_count), "lane", scatter_dimension=0, tiled=True
    )
    return direct + owned


def solution(mesh):
    return jax.shard_map(
        shards,
        mesh=mesh,
        in_specs=(
            P(None, ("blk", "lane")),
            P(None, ("blk", "lane")),
            P(None, ("blk", "lane")),
            P(None, ("blk", "lane")),
            P(("blk", "lane")),
            P(("blk", "lane")),
            P(("blk", "lane"), None),
            P(("blk", "lane"), None),
            P("blk", "lane", None, None, None),
            P("blk", "lane", None, None),
        ),
        out_specs=P(("blk", "lane"), None),
        check_vma=False,
    )
```

profile of v0, /device:TPU:2, one launch (start us, length us, event | category | flops | bytes accessed | tf_op | source)
XLA Modules:
  0.0 2028.8 jit_solution(4897555335530008646)
XLA Ops:
  7.5 562.1 %all_gather.6 = f32[2,32768]{1,0:T(2,128)S(1)} all-gather(f32[2,128]{1,0:T(2,128)} %param.15), channel_id=1, replica_groups=mesh['blk'=16,'lane'=16] {'blk','lane'}, dimensions={1}, use_global_device_ids=true | all-gather | bytes 263168 | tf_op jit(solution)/shard_map/all_gather | solution.py:56
  577.1 593.8 %all_gather.7 = f32[3,32768]{1,0:T(4,128)} all-gather(f32[3,128]{1,0:T(4,128)} %param.14), channel_id=1, replica_groups=mesh['blk'=16,'lane'=16] {'blk','lane'}, dimensions={1}, use_global_device_ids=true | all-gather | bytes 394752 | tf_op jit(solution)/shard_map/all_gather | solution.py:55
  1184.7 602.5 %while.17 = (s32[]{:T(128)}, f32[16,128,128]{2,1,0:T(8,128)}, s32[]{:T(128)}, s32[16,16]{1,0:T(8,128)S(1)}, s32[16,16,4]{2,1,0:T(8,128)S(1)}, /*index=5*/f32[8,1...) while((s32[]{:T(128)}, f32[16,128,128]{2,1,0:T(8,128)}, ...), condition=%wide.region_1.3_spmd.clone.clone, body=%wide.region_0.2_spmd.clone.clone.sunk | while | flops 299129344 | bytes 18412892 | solution.py:106
  1192.4 8.1 fusion.118
  1200.7 39.9 %collective-permute-done = f32[16,128,128]{2,1,0:T(8,128)S(1)} collective-permute-done((f32[16,128,128]{2,1,0:T(8,128)}, f32[16,128,128]{2,1,0:T(8,128)S(1)}, u32[]{:S(2)}, u32[]{:S(2)}) %collective-permute-start) | collective-permute-done | bytes 1048608 | tf_op jit(solution)/shard_map/while/body/eval_jaxpr/ppermute | solution.py:10
  1249.2 8.1 fusion.118
  1257.3 34.7 %collective-permute-done = f32[16,128,128]{2,1,0:T(8,128)S(1)} collective-permute-done((f32[16,128,128]{2,1,0:T(8,128)}, f32[16,128,128]{2,1,0:T(8,128)S(1)}, u32[]{:S(2)}, u32[]{:S(2)}) %collective-permute-start) | collective-permute-done | bytes 1048608 | tf_op jit(solution)/shard_map/while/body/eval_jaxpr/ppermute | solution.py:10
  1300.7 8.1 fusion.118
  1308.8 59.2 %collective-permute-done = f32[16,128,128]{2,1,0:T(8,128)S(1)} collective-permute-done((f32[16,128,128]{2,1,0:T(8,128)}, f32[16,128,128]{2,1,0:T(8,128)S(1)}, u32[]{:S(2)}, u32[]{:S(2)}) %collective-permute-start) | collective-permute-done | bytes 1048608 | tf_op jit(solution)/shard_map/while/body/eval_jaxpr/ppermute | solution.py:10
  1384.9 34.7 %collective-permute-done = f32[16,128,128]{2,1,0:T(8,128)S(1)} collective-permute-done((f32[16,128,128]{2,1,0:T(8,128)}, f32[16,128,128]{2,1,0:T(8,128)S(1)}, u32[]{:S(2)}, u32[]{:S(2)}) %collective-permute-start) | collective-permute-done | bytes 1048608 | tf_op jit(solution)/shard_map/while/body/eval_jaxpr/ppermute | solution.py:10
  1436.4 16.5 collective-permute-done
  1469.7 16.5 collective-permute-done
  1494.9 8.1 fusion.118
  1503.0 16.6 collective-permute-done
  1536.4 16.5 collective-permute-done
  1569.7 16.5 collective-permute-done
  1603.0 16.5 collective-permute-done
  1636.4 16.5 collective-permute-done
  1669.7 16.5 collective-permute-done
  1703.0 16.5 collective-permute-done
  1728.3 8.1 fusion.118
  1736.4 16.5 collective-permute-done
  1769.7 16.5 collective-permute-done
  1794.5 225.9 %reduce-scatter.2.cloned.1.call-done = f32[128,128]{1,0:T(8,128)} async-done(((f32[2048,128]{1,0:T(8,128)}), f32[128,128]{1,0:T(8,128)}) %reduce-scatter.2.cloned.1.call-update) | async-done | bytes 65552 | tf_op jit(solution)/shard_map/reduce_scatter | solution.py:108
  (463 shorter events, 241.1 us)
Async XLA Ops:
  6.5 1166.3 %copy-start.1 = (bf16[1024,128]{1,0:T(8,128)(2,1)S(1)}, bf16[1024,128]{1,0:T(8,128)(2,1)}, u32[]{:S(2)}) copy-start(bf16[1024,128]{1,0:T(8,128)(2,1)} %param.20) | copy-start | bytes 786436
  6.5 2013.9 %reduce-scatter.2.cloned.1.call-start = ((), (), s32[]{:S(2)}) async-start(), calls=%async_computation.1 | async-start | bytes 1114112 | tf_op jit(solution)/shard_map/reduce_scatter | solution.py:108
  1172.8 2.2 copy-start.3
  1172.8 6.7 copy-start.4
  1175.0 5.9 copy-start.2
  1175.0 6.5 copy-start
  1175.6 9.1 copy-start.6
  1200.5 40.0 %collective-permute-start = (f32[16,128,128]{2,1,0:T(8,128)}, f32[16,128,128]{2,1,0:T(8,128)S(1)}, u32[]{:S(2)}, u32[]{:S(2)}) collective-permute-start(f32[16,128,128]{2,1,0:T(8,128)} %fusion.118), channel_id=1, source_target_pairs={{240,0},{0,16},{16,32},{32,48},{48,64},{64,80},{80,96},{96,112},{1... | collective-permute-start | bytes 3145736 | tf_op jit(solution)/shard_map/while/body/eval_jaxpr/ppermute | solution.py:10
  1240.5 1.0 copy-start.5
  1257.3 34.7 %collective-permute-start = (f32[16,128,128]{2,1,0:T(8,128)}, f32[16,128,128]{2,1,0:T(8,128)S(1)}, u32[]{:S(2)}, u32[]{:S(2)}) collective-permute-start(f32[16,128,128]{2,1,0:T(8,128)} %fusion.118), channel_id=1, source_target_pairs={{240,0},{0,16},{16,32},{32,48},{48,64},{64,80},{80,96},{96,112},{1... | collective-permute-start | bytes 3145736 | tf_op jit(solution)/shard_map/while/body/eval_jaxpr/ppermute | solution.py:10
  1308.8 59.3 %collective-permute-start = (f32[16,128,128]{2,1,0:T(8,128)}, f32[16,128,128]{2,1,0:T(8,128)S(1)}, u32[]{:S(2)}, u32[]{:S(2)}) collective-permute-start(f32[16,128,128]{2,1,0:T(8,128)} %fusion.118), channel_id=1, source_target_pairs={{240,0},{0,16},{16,32},{32,48},{48,64},{64,80},{80,96},{96,112},{1... | collective-permute-start | bytes 3145736 | tf_op jit(solution)/shard_map/while/body/eval_jaxpr/ppermute | solution.py:10
  1384.9 34.7 %collective-permute-start = (f32[16,128,128]{2,1,0:T(8,128)}, f32[16,128,128]{2,1,0:T(8,128)S(1)}, u32[]{:S(2)}, u32[]{:S(2)}) collective-permute-start(f32[16,128,128]{2,1,0:T(8,128)} %fusion.118), channel_id=1, source_target_pairs={{240,0},{0,16},{16,32},{32,48},{48,64},{64,80},{80,96},{96,112},{1... | collective-permute-start | bytes 3145736 | tf_op jit(solution)/shard_map/while/body/eval_jaxpr/ppermute | solution.py:10
  1436.4 16.5 collective-permute-start
  1469.7 16.5 collective-permute-start
  1503.0 16.6 collective-permute-start
  1536.4 16.5 collective-permute-start
  1569.7 16.6 collective-permute-start
  1603.0 16.5 collective-permute-start
  1636.4 16.5 collective-permute-start
  1669.7 16.5 collective-permute-start
  1703.0 16.6 collective-permute-start
  1736.4 16.5 collective-permute-start
  1769.7 16.5 collective-permute-start
  1787.2 233.2 %copy-start.7 = (f32[128,128]{1,0:T(8,128)S(1)}, f32[128,128]{1,0:T(8,128)}, u32[]{:S(2)}) copy-start(f32[128,128]{1,0:T(8,128)} %param.21) | copy-start | bytes 196612
  (14 other events, 13.9 us)
Sparse Core Ops, SparseCore 0:
  1794.7 225.7 reduce-scatter.1
where the time goes:
time: 2030 us
  blocking collectives  1160 us (57%)
  waiting for transfers between devices  576 us (28%)
  local copies, waits for them, and re-layouts  138 us (7%)
  matrix products  129 us (6%)
    all_gather x1, blocking collectives, shards(): lax.all_gather(recv_pos, ('blk', 'lane'), axis=1, tiled=True)  594 us
    all_gather x1, blocking collectives, shards(): lax.all_gather(recv_angles, ('blk', 'lane'), axis=1, tiled=True)  562 us
    ppermute x15, waiting for transfers between devices, shifted(): return lax.ppermute(block, axis, route)  350 us
    reduce_scatter x1, waiting for transfers between devices, shards(): lax.psum_scatter(running.reshape(lane_count * block_rows, bin_count), 'la...  226 us
    dot_general x16, matrix products, contribution(): jnp.einsum('jrcs,jcsb->jrb', values, picked_flux, preferred_element_type=...  129 us
  transfers between devices with their start and end apart: 16, of which 16 were waited for; matrix products, arithmetic and copies ran while one was open for 0% of the time, Pallas kernels for 0%

commit v1 on v0

--- a/solution.py
+++ b/solution.py
@@ -52,7 +52,12 @@
     source_blocks = src_area.shape[0] // block_rows
     slot_count = visible_lists.shape[-1]
     every_pos, every_angles = (
-        lax.all_gather(recv_pos, ("blk", "lane"), axis=1, tiled=True),
+        jnp.concatenate(
+            lax.all_to_all(
+                jnp.stack([recv_pos] * lax.axis_size(("blk", "lane"))), ("blk", "lane"), 0, 0
+            ),
+            axis=1,
+        ),
         lax.all_gather(recv_angles, ("blk", "lane"), axis=1, tiled=True),
     )
     receiver_pos = every_pos.reshape(3, group_count * lane_count, block_rows)

time: 2030 us -> 1380 us (0.68)
  blocking collectives: 1160 us -> 562 us
  waiting for transfers between devices: 576 us -> 505 us
    all_gather x1 -> x0, blocking collectives: 594 us -> none  [shards(): lax.all_gather(recv_pos, ('blk', 'lane'), axis=1, tiled=True)]
    ppermute x15, waiting for transfers between devices: 350 us -> 281 us  [shifted(): return lax.ppermute(block, axis, route)]
  transfers between devices with their start and end apart: 16 -> 17, of which waited for: 16 -> 16; matrix products, arithmetic and copies ran while one was open for 0% -> 1% of each run, Pallas kernels for 0% -> 0%
where the time goes in v1:
time: 1380 us
  blocking collectives  562 us (41%)
  waiting for transfers between devices  505 us (37%)
  local copies, waits for them, and re-layouts  139 us (10%)
  matrix products  129 us (9%)
  starting transfers between devices  15.8 us (1%)
    all_gather x1, blocking collectives, shards(): lax.all_gather(recv_angles, ('blk', 'lane'), axis=1, tiled=True)  562 us
    ppermute x15, waiting for transfers between devices, shifted(): return lax.ppermute(block, axis, route)  281 us
    reduce_scatter x1, waiting for transfers between devices, shards(): lax.psum_scatter(running.reshape(lane_count * block_rows, bin_count), 'la...  224 us
    dot_general x16, matrix products, contribution(): jnp.einsum('jrcs,jcsb->jrb', values, picked_flux, preferred_element_type=...  129 us
  transfers between devices with their start and end apart: 17, of which 16 were waited for; matrix products, arithmetic and copies ran while one was open for 1% of the time, Pallas kernels for 0%

profile of v1, /device:TPU:2, one launch (start us, length us, event | category | flops | bytes accessed | tf_op | source)
XLA Modules:
  0.0 1379.7 jit_solution(9884438744896925294)
XLA Ops:
  8.1 15.7 %all-to-all-start = ((f32[256,3,128]{2,1,0:T(4,128)}), f32[256,3,128]{2,1,0:T(4,128)}, u32[]{:S(2)}, u32[]{:S(2)}) async-start(f32[256,3,128]{2,1,0:T(4,128)} %stack.22), calls=%async_computation | async-start | bytes 1048576 | tf_op jit(solution)/shard_map/all_to_all | solution.py:56
  24.8 561.8 %all_gather.3 = f32[2,32768]{1,0:T(2,128)S(1)} all-gather(f32[2,128]{1,0:T(2,128)} %param.15), channel_id=1, replica_groups=mesh['blk'=16,'lane'=16] {'blk','lane'}, dimensions={1}, use_global_device_ids=true | all-gather | bytes 263168 | tf_op jit(solution)/shard_map/all_gather | solution.py:61
  607.2 533.0 %while.17 = (s32[]{:T(128)}, f32[16,128,128]{2,1,0:T(8,128)}, s32[]{:T(128)}, s32[16,16]{1,0:T(8,128)S(1)}, s32[16,16,4]{2,1,0:T(8,128)S(1)}, /*index=5*/f32[8,1...) while((s32[]{:T(128)}, f32[16,128,128]{2,1,0:T(8,128)}, ...), condition=%wide.region_1.3_spmd.clone.clone, body=%wide.region_0.2_spmd.clone.clone.sunk | while | flops 299129344 | bytes 18412892 | solution.py:111
  614.9 8.1 fusion.118
  623.0 15.3 %collective-permute-done = f32[16,128,128]{2,1,0:T(8,128)S(1)} collective-permute-done((f32[16,128,128]{2,1,0:T(8,128)}, f32[16,128,128]{2,1,0:T(8,128)S(1)}, u32[]{:S(2)}, u32[]{:S(2)}) %collective-permute-start) | collective-permute-done | bytes 1048608 | tf_op jit(solution)/shard_map/while/body/eval_jaxpr/ppermute | solution.py:10
  655.1 15.3 %collective-permute-done = f32[16,128,128]{2,1,0:T(8,128)S(1)} collective-permute-done((f32[16,128,128]{2,1,0:T(8,128)}, f32[16,128,128]{2,1,0:T(8,128)S(1)}, u32[]{:S(2)}, u32[]{:S(2)}) %collective-permute-start) | collective-permute-done | bytes 1048608 | tf_op jit(solution)/shard_map/while/body/eval_jaxpr/ppermute | solution.py:10
  687.2 34.1 %collective-permute-done = f32[16,128,128]{2,1,0:T(8,128)S(1)} collective-permute-done((f32[16,128,128]{2,1,0:T(8,128)}, f32[16,128,128]{2,1,0:T(8,128)S(1)}, u32[]{:S(2)}, u32[]{:S(2)}) %collective-permute-start) | collective-permute-done | bytes 1048608 | tf_op jit(solution)/shard_map/while/body/eval_jaxpr/ppermute | solution.py:10
  738.1 34.7 %collective-permute-done = f32[16,128,128]{2,1,0:T(8,128)S(1)} collective-permute-done((f32[16,128,128]{2,1,0:T(8,128)}, f32[16,128,128]{2,1,0:T(8,128)S(1)}, u32[]{:S(2)}, u32[]{:S(2)}) %collective-permute-start) | collective-permute-done | bytes 1048608 | tf_op jit(solution)/shard_map/while/body/eval_jaxpr/ppermute | solution.py:10
  789.6 16.5 %collective-permute-done = f32[16,128,128]{2,1,0:T(8,128)S(1)} collective-permute-done((f32[16,128,128]{2,1,0:T(8,128)}, f32[16,128,128]{2,1,0:T(8,128)S(1)}, u32[]{:S(2)}, u32[]{:S(2)}) %collective-permute-start) | collective-permute-done | bytes 1048608 | tf_op jit(solution)/shard_map/while/body/eval_jaxpr/ppermute | solution.py:10
  814.8 8.1 fusion.118
  822.9 16.5 %collective-permute-done = f32[16,128,128]{2,1,0:T(8,128)S(1)} collective-permute-done((f32[16,128,128]{2,1,0:T(8,128)}, f32[16,128,128]{2,1,0:T(8,128)S(1)}, u32[]{:S(2)}, u32[]{:S(2)}) %collective-permute-start) | collective-permute-done | bytes 1048608 | tf_op jit(solution)/shard_map/while/body/eval_jaxpr/ppermute | solution.py:10
  848.1 8.1 fusion.118
  856.2 16.6 %collective-permute-done = f32[16,128,128]{2,1,0:T(8,128)S(1)} collective-permute-done((f32[16,128,128]{2,1,0:T(8,128)}, f32[16,128,128]{2,1,0:T(8,128)S(1)}, u32[]{:S(2)}, u32[]{:S(2)}) %collective-permute-start) | collective-permute-done | bytes 1048608 | tf_op jit(solution)/shard_map/while/body/eval_jaxpr/ppermute | solution.py:10
  881.4 8.1 fusion.118
  889.5 16.5 %collective-permute-done = f32[16,128,128]{2,1,0:T(8,128)S(1)} collective-permute-done((f32[16,128,128]{2,1,0:T(8,128)}, f32[16,128,128]{2,1,0:T(8,128)S(1)}, u32[]{:S(2)}, u32[]{:S(2)}) %collective-permute-start) | collective-permute-done | bytes 1048608 | tf_op jit(solution)/shard_map/while/body/eval_jaxpr/ppermute | solution.py:10
  922.8 16.5 %collective-permute-done = f32[16,128,128]{2,1,0:T(8,128)S(1)} collective-permute-done((f32[16,128,128]{2,1,0:T(8,128)}, f32[16,128,128]{2,1,0:T(8,128)S(1)}, u32[]{:S(2)}, u32[]{:S(2)}) %collective-permute-start) | collective-permute-done | bytes 1048608 | tf_op jit(solution)/shard_map/while/body/eval_jaxpr/ppermute | solution.py:10
  956.1 16.5 %collective-permute-done = f32[16,128,128]{2,1,0:T(8,128)S(1)} collective-permute-done((f32[16,128,128]{2,1,0:T(8,128)}, f32[16,128,128]{2,1,0:T(8,128)S(1)}, u32[]{:S(2)}, u32[]{:S(2)}) %collective-permute-start) | collective-permute-done | bytes 1048608 | tf_op jit(solution)/shard_map/while/body/eval_jaxpr/ppermute | solution.py:10
  989.5 16.5 %collective-permute-done = f32[16,128,128]{2,1,0:T(8,128)S(1)} collective-permute-done((f32[16,128,128]{2,1,0:T(8,128)}, f32[16,128,128]{2,1,0:T(8,128)S(1)}, u32[]{:S(2)}, u32[]{:S(2)}) %collective-permute-start) | collective-permute-done | bytes 1048608 | tf_op jit(solution)/shard_map/while/body/eval_jaxpr/ppermute | solution.py:10
  1022.8 16.5 %collective-permute-done = f32[16,128,128]{2,1,0:T(8,128)S(1)} collective-permute-done((f32[16,128,128]{2,1,0:T(8,128)}, f32[16,128,128]{2,1,0:T(8,128)S(1)}, u32[]{:S(2)}, u32[]{:S(2)}) %collective-permute-start) | collective-permute-done | bytes 1048608 | tf_op jit(solution)/shard_map/while/body/eval_jaxpr/ppermute | solution.py:10
  1048.0 8.1 fusion.118
  1056.1 16.5 %collective-permute-done = f32[16,128,128]{2,1,0:T(8,128)S(1)} collective-permute-done((f32[16,128,128]{2,1,0:T(8,128)}, f32[16,128,128]{2,1,0:T(8,128)S(1)}, u32[]{:S(2)}, u32[]{:S(2)}) %collective-permute-start) | collective-permute-done | bytes 1048608 | tf_op jit(solution)/shard_map/while/body/eval_jaxpr/ppermute | solution.py:10
  1089.4 16.5 %collective-permute-done = f32[16,128,128]{2,1,0:T(8,128)S(1)} collective-permute-done((f32[16,128,128]{2,1,0:T(8,128)}, f32[16,128,128]{2,1,0:T(8,128)S(1)}, u32[]{:S(2)}, u32[]{:S(2)}) %collective-permute-start) | collective-permute-done | bytes 1048608 | tf_op jit(solution)/shard_map/while/body/eval_jaxpr/ppermute | solution.py:10
  1122.7 16.5 %collective-permute-done = f32[16,128,128]{2,1,0:T(8,128)S(1)} collective-permute-done((f32[16,128,128]{2,1,0:T(8,128)}, f32[16,128,128]{2,1,0:T(8,128)S(1)}, u32[]{:S(2)}, u32[]{:S(2)}) %collective-permute-start) | collective-permute-done | bytes 1048608 | tf_op jit(solution)/shard_map/while/body/eval_jaxpr/ppermute | solution.py:10
  1147.5 223.9 %reduce-scatter.2.cloned.1.call-done = f32[128,128]{1,0:T(8,128)} async-done(((f32[2048,128]{1,0:T(8,128)}), f32[128,128]{1,0:T(8,128)}) %reduce-scatter.2.cloned.1.call-update) | async-done | bytes 65552 | tf_op jit(solution)/shard_map/reduce_scatter | solution.py:113
  (467 shorter events, 241.3 us)
Async XLA Ops:
  6.5 587.6 %copy-start.8 = (f32[2,1024]{1,0:T(2,128)S(1)}, f32[2,1024]{1,0:T(2,128)}, u32[]{:S(2)}) copy-start(f32[2,1024]{1,0:T(2,128)} %param.17) | copy-start | bytes 24580
  6.5 588.8 %copy-start.1 = (bf16[1024,128]{1,0:T(8,128)(2,1)S(1)}, bf16[1024,128]{1,0:T(8,128)(2,1)}, u32[]{:S(2)}) copy-start(bf16[1024,128]{1,0:T(8,128)(2,1)} %param.20) | copy-start | bytes 786436
  8.1 595.7 %all-to-all-start = ((f32[256,3,128]{2,1,0:T(4,128)}), f32[256,3,128]{2,1,0:T(4,128)}, u32[]{:S(2)}, u32[]{:S(2)}) async-start(f32[256,3,128]{2,1,0:T(4,128)} %stack.22), calls=%async_computation | async-start | bytes 1048576 | tf_op jit(solution)/shard_map/all_to_all | solution.py:56
  23.8 1347.6 %reduce-scatter.2.cloned.1.call-start = ((), (), s32[]{:S(2)}) async-start(), calls=%async_computation.2 | async-start | bytes 1114112 | tf_op jit(solution)/shard_map/reduce_scatter | solution.py:113
  595.3 3.5 copy-start.4
  595.3 4.2 copy-start.2
  595.3 4.8 copy-start
  598.1 9.1 copy-start.6
  623.0 15.3 %collective-permute-start = (f32[16,128,128]{2,1,0:T(8,128)}, f32[16,128,128]{2,1,0:T(8,128)S(1)}, u32[]{:S(2)}, u32[]{:S(2)}) collective-permute-start(f32[16,128,128]{2,1,0:T(8,128)} %fusion.118), channel_id=1, source_target_pairs={{240,0},{0,16},{16,32},{32,48},{48,64},{64,80},{80,96},{96,112},{1... | collective-permute-start | bytes 3145736 | tf_op jit(solution)/shard_map/while/body/eval_jaxpr/ppermute | solution.py:10
  655.1 15.3 %collective-permute-start = (f32[16,128,128]{2,1,0:T(8,128)}, f32[16,128,128]{2,1,0:T(8,128)S(1)}, u32[]{:S(2)}, u32[]{:S(2)}) collective-permute-start(f32[16,128,128]{2,1,0:T(8,128)} %fusion.118), channel_id=1, source_target_pairs={{240,0},{0,16},{16,32},{32,48},{48,64},{64,80},{80,96},{96,112},{1... | collective-permute-start | bytes 3145736 | tf_op jit(solution)/shard_map/while/body/eval_jaxpr/ppermute | solution.py:10
  687.2 34.1 %collective-permute-start = (f32[16,128,128]{2,1,0:T(8,128)}, f32[16,128,128]{2,1,0:T(8,128)S(1)}, u32[]{:S(2)}, u32[]{:S(2)}) collective-permute-start(f32[16,128,128]{2,1,0:T(8,128)} %fusion.118), channel_id=1, source_target_pairs={{240,0},{0,16},{16,32},{32,48},{48,64},{64,80},{80,96},{96,112},{1... | collective-permute-start | bytes 3145736 | tf_op jit(solution)/shard_map/while/body/eval_jaxpr/ppermute | solution.py:10
  738.1 34.7 %collective-permute-start = (f32[16,128,128]{2,1,0:T(8,128)}, f32[16,128,128]{2,1,0:T(8,128)S(1)}, u32[]{:S(2)}, u32[]{:S(2)}) collective-permute-start(f32[16,128,128]{2,1,0:T(8,128)} %fusion.118), channel_id=1, source_target_pairs={{240,0},{0,16},{16,32},{32,48},{48,64},{64,80},{80,96},{96,112},{1... | collective-permute-start | bytes 3145736 | tf_op jit(solution)/shard_map/while/body/eval_jaxpr/ppermute | solution.py:10
  789.6 16.5 %collective-permute-start = (f32[16,128,128]{2,1,0:T(8,128)}, f32[16,128,128]{2,1,0:T(8,128)S(1)}, u32[]{:S(2)}, u32[]{:S(2)}) collective-permute-start(f32[16,128,128]{2,1,0:T(8,128)} %fusion.118), channel_id=1, source_target_pairs={{240,0},{0,16},{16,32},{32,48},{48,64},{64,80},{80,96},{96,112},{1... | collective-permute-start | bytes 3145736 | tf_op jit(solution)/shard_map/while/body/eval_jaxpr/ppermute | solution.py:10
  822.9 16.5 %collective-permute-start = (f32[16,128,128]{2,1,0:T(8,128)}, f32[16,128,128]{2,1,0:T(8,128)S(1)}, u32[]{:S(2)}, u32[]{:S(2)}) collective-permute-start(f32[16,128,128]{2,1,0:T(8,128)} %fusion.118), channel_id=1, source_target_pairs={{240,0},{0,16},{16,32},{32,48},{48,64},{64,80},{80,96},{96,112},{1... | collective-permute-start | bytes 3145736 | tf_op jit(solution)/shard_map/while/body/eval_jaxpr/ppermute | solution.py:10
  856.2 16.6 %collective-permute-start = (f32[16,128,128]{2,1,0:T(8,128)}, f32[16,128,128]{2,1,0:T(8,128)S(1)}, u32[]{:S(2)}, u32[]{:S(2)}) collective-permute-start(f32[16,128,128]{2,1,0:T(8,128)} %fusion.118), channel_id=1, source_target_pairs={{240,0},{0,16},{16,32},{32,48},{48,64},{64,80},{80,96},{96,112},{1... | collective-permute-start | bytes 3145736 | tf_op jit(solution)/shard_map/while/body/eval_jaxpr/ppermute | solution.py:10
  889.5 16.5 %collective-permute-start = (f32[16,128,128]{2,1,0:T(8,128)}, f32[16,128,128]{2,1,0:T(8,128)S(1)}, u32[]{:S(2)}, u32[]{:S(2)}) collective-permute-start(f32[16,128,128]{2,1,0:T(8,128)} %fusion.118), channel_id=1, source_target_pairs={{240,0},{0,16},{16,32},{32,48},{48,64},{64,80},{80,96},{96,112},{1... | collective-permute-start | bytes 3145736 | tf_op jit(solution)/shard_map/while/body/eval_jaxpr/ppermute | solution.py:10
  922.8 16.6 %collective-permute-start = (f32[16,128,128]{2,1,0:T(8,128)}, f32[16,128,128]{2,1,0:T(8,128)S(1)}, u32[]{:S(2)}, u32[]{:S(2)}) collective-permute-start(f32[16,128,128]{2,1,0:T(8,128)} %fusion.118), channel_id=1, source_target_pairs={{240,0},{0,16},{16,32},{32,48},{48,64},{64,80},{80,96},{96,112},{1... | collective-permute-start | bytes 3145736 | tf_op jit(solution)/shard_map/while/body/eval_jaxpr/ppermute | solution.py:10
  956.1 16.5 %collective-permute-start = (f32[16,128,128]{2,1,0:T(8,128)}, f32[16,128,128]{2,1,0:T(8,128)S(1)}, u32[]{:S(2)}, u32[]{:S(2)}) collective-permute-start(f32[16,128,128]{2,1,0:T(8,128)} %fusion.118), channel_id=1, source_target_pairs={{240,0},{0,16},{16,32},{32,48},{48,64},{64,80},{80,96},{96,112},{1... | collective-permute-start | bytes 3145736 | tf_op jit(solution)/shard_map/while/body/eval_jaxpr/ppermute | solution.py:10
  989.5 16.5 %collective-permute-start = (f32[16,128,128]{2,1,0:T(8,128)}, f32[16,128,128]{2,1,0:T(8,128)S(1)}, u32[]{:S(2)}, u32[]{:S(2)}) collective-permute-start(f32[16,128,128]{2,1,0:T(8,128)} %fusion.118), channel_id=1, source_target_pairs={{240,0},{0,16},{16,32},{32,48},{48,64},{64,80},{80,96},{96,112},{1... | collective-permute-start | bytes 3145736 | tf_op jit(solution)/shard_map/while/body/eval_jaxpr/ppermute | solution.py:10
  1022.8 16.5 %collective-permute-start = (f32[16,128,128]{2,1,0:T(8,128)}, f32[16,128,128]{2,1,0:T(8,128)S(1)}, u32[]{:S(2)}, u32[]{:S(2)}) collective-permute-start(f32[16,128,128]{2,1,0:T(8,128)} %fusion.118), channel_id=1, source_target_pairs={{240,0},{0,16},{16,32},{32,48},{48,64},{64,80},{80,96},{96,112},{1... | collective-permute-start | bytes 3145736 | tf_op jit(solution)/shard_map/while/body/eval_jaxpr/ppermute | solution.py:10
  1056.1 16.6 %collective-permute-start = (f32[16,128,128]{2,1,0:T(8,128)}, f32[16,128,128]{2,1,0:T(8,128)S(1)}, u32[]{:S(2)}, u32[]{:S(2)}) collective-permute-start(f32[16,128,128]{2,1,0:T(8,128)} %fusion.118), channel_id=1, source_target_pairs={{240,0},{0,16},{16,32},{32,48},{48,64},{64,80},{80,96},{96,112},{1... | collective-permute-start | bytes 3145736 | tf_op jit(solution)/shard_map/while/body/eval_jaxpr/ppermute | solution.py:10
  1089.4 16.5 %collective-permute-start = (f32[16,128,128]{2,1,0:T(8,128)}, f32[16,128,128]{2,1,0:T(8,128)S(1)}, u32[]{:S(2)}, u32[]{:S(2)}) collective-permute-start(f32[16,128,128]{2,1,0:T(8,128)} %fusion.118), channel_id=1, source_target_pairs={{240,0},{0,16},{16,32},{32,48},{48,64},{64,80},{80,96},{96,112},{1... | collective-permute-start | bytes 3145736 | tf_op jit(solution)/shard_map/while/body/eval_jaxpr/ppermute | solution.py:10
  1122.7 16.5 %collective-permute-start = (f32[16,128,128]{2,1,0:T(8,128)}, f32[16,128,128]{2,1,0:T(8,128)S(1)}, u32[]{:S(2)}, u32[]{:S(2)}) collective-permute-start(f32[16,128,128]{2,1,0:T(8,128)} %fusion.118), channel_id=1, source_target_pairs={{240,0},{0,16},{16,32},{32,48},{48,64},{64,80},{80,96},{96,112},{1... | collective-permute-start | bytes 3145736 | tf_op jit(solution)/shard_map/while/body/eval_jaxpr/ppermute | solution.py:10
  1140.2 231.2 %copy-start.7 = (f32[128,128]{1,0:T(8,128)S(1)}, f32[128,128]{1,0:T(8,128)}, u32[]{:S(2)}) copy-start(f32[128,128]{1,0:T(8,128)} %param.21) | copy-start | bytes 196612
  (16 other events, 16.6 us)
Sparse Core Ops, SparseCore 0:
  1147.6 223.7 reduce-scatter.1
